TPU v7x, 256 devices: a whole 4x4x8 slice. The times are simulated.
256 devices in a mesh: dom: 8 (over y, core), shard: 32 (over x, z).
Axes of the slice: x: 4, y: 4, z: 8, core: 2. Of those that a mesh axis runs over, the one named last changes fastest.
Arguments:
- features: bfloat16 [65536, 512], P(('dom', 'shard')), may hold values from -6 to 6
- w_self: bfloat16 [512, 512], replicated, may hold values from -0.25 to 0.25
- w_neigh: bfloat16 [512, 512], replicated, may hold values from -0.25 to 0.25
- cotangent: bfloat16 [65536, 512], P(('dom', 'shard')), may hold values from -6 to 6
- neighbours: int32 [65536, 32], P(('dom', 'shard')), may hold values from 0 to 640, as said below
- hub_slots: int32 [256], P(('dom', 'shard')), may hold values from 0 to 255, as said below
- send_rows: int32 [256, 32, 4], P(('dom', 'shard')), may hold values from 0 to 255, as said below
- send_counts: int32 [256, 32], P(('dom', 'shard')), may hold values from 1 to 4, as said below
Outputs:
- hidden: bfloat16 [65536, 512], P(('dom', 'shard'))
- grad_features: float32 [65536, 512], P(('dom', 'shard'))
- grad_self: float32 [512, 512], replicated
- grad_neigh: float32 [512, 512], replicated
Inputs may be any that keep to these rules, and one draw needn't show every extreme that they name: `neighbours`: padding slots (640) come after a vertex's live slots; each vertex has 4 to 32 live slots. A slot at or above 512 names peer p and position k with k below send_counts of that peer for this device. Hub indices are skewed: some hubs are read far more than others. `hub_slots`: the 1 entries of one device are distinct local rows. `send_rows`: rows may repeat; entries at or past a peer's count are not live. `send_counts`: in every partition group one shard index receives 4 rows from every peer.
All inputs are finite; a program needn't handle non-finite values.
Results may differ from a plain program's by a relative error of at most 0.0052.
Values may be sent and summed in bfloat16 or wider, within the bound.
No kernel may reach another device: no remote copies, remote signals or barrier semaphores. Data moves between devices by JAX's collectives and lax.ppermute only.
A program may use at most 64 MiB of HBM per device.

v0:
```python
import jax
import jax.numpy as jnp
from jax import lax
from jax.sharding import PartitionSpec as P

row_block = 128


def contract_rows(left, right):
    return lax.dot_general(
        left, right, (((0,), (0,)), ((), ())), preferred_element_type=jnp.float32
    )


def contract_cols(left, right):
    return lax.dot_general(
        left, right, (((1,), (1,)), ((), ())), preferred_element_type=jnp.float32
    )


def body(features, w_self, w_neigh, cotangent, neighbours, hub_slots, send_rows, send_counts):
    verts, width = features.shape
    slots = neighbours.shape[1]
    peers = lax.axis_size("shard")
    routes = send_rows[0]
    counts = send_counts[0]
    cap = routes.shape[1]
    live = jnp.arange(cap)[None, :] < counts[:, None]
    hub_local = features[hub_slots]
    hubs = lax.all_gather(hub_local, ("dom", "shard"), axis=0, tiled=True)
    outgoing = jnp.where(live[:, :, None], features[routes], jnp.zeros((), jnp.bfloat16))
    incoming = lax.all_to_all(outgoing, "shard", split_axis=0, concat_axis=0, tiled=True)
    hub_count = hubs.shape[0]
    table_size = verts + hub_count + peers * cap
    table = jnp.concatenate(
        [features, hubs, incoming.reshape(peers * cap, width), jnp.zeros((1, width), jnp.bfloat16)],
        axis=0,
    )
    degree = jnp.sum(neighbours < table_size, axis=1).astype(jnp.float32)
    blocks = neighbours.reshape(verts // row_block, row_block, slots)
    sums = lax.map(lambda blk: jnp.sum(table[blk], axis=1, dtype=jnp.float32), blocks).reshape(
        verts, width
    )
    agg = (sums / degree[:, None]).astype(jnp.bfloat16)
    z = jnp.dot(features, w_self, preferred_element_type=jnp.float32) + jnp.dot(
        agg, w_neigh, preferred_element_type=jnp.float32
    )
    sig = jax.nn.sigmoid(z)
    hidden = (z * sig).astype(jnp.bfloat16)
    dz = (cotangent.astype(jnp.float32) * sig * (1.0 + z * (1.0 - sig))).astype(jnp.bfloat16)
    grad_self, grad_neigh = lax.psum(
        (contract_rows(features, dz), contract_rows(agg, dz)), ("dom", "shard")
    )
    edge_grad = contract_cols(dz, w_neigh) / degree[:, None]
    grads = edge_grad.reshape(verts // row_block, row_block, width)

    def add_block(acc, pair):
        blk, grad = pair
        spread = jnp.broadcast_to(grad[:, None, :], (row_block, slots, width)).reshape(-1, width)
        return (acc.at[blk.reshape(-1)].add(spread), None)

    start = jnp.zeros((table_size + 1, width), jnp.float32)
    accum, _ = lax.scan(add_block, start, (blocks, grads))
    hub_part = accum[verts : verts + hub_count]
    hub_back = lax.psum_scatter(hub_part, ("dom", "shard"), scatter_dimension=0, tiled=True)
    recv_part = accum[verts + hub_count : table_size].reshape(peers, cap, width)
    returned = lax.all_to_all(
        recv_part.astype(jnp.bfloat16), "shard", split_axis=0, concat_axis=0, tiled=True
    ).astype(recv_part.dtype)
    returned = jnp.where(live[:, :, None], returned, 0.0)
    grad_features = contract_cols(dz, w_self) + accum[:verts]
    grad_features = grad_features.at[hub_slots].add(hub_back)
    grad_features = grad_features.at[routes.reshape(-1)].add(returned.reshape(-1, width))
    return (hidden, grad_features, grad_self, grad_neigh)


def solution(mesh):
    return jax.shard_map(
        body,
        mesh=mesh,
        in_specs=(
            P(("dom", "shard"), None),
            P(),
            P(),
            P(("dom", "shard"), None),
            P(("dom", "shard"), None),
            P(("dom", "shard")),
            P(("dom", "shard"), None, None),
            P(("dom", "shard"), None),
        ),
        out_specs=(P(("dom", "shard"), None), P(("dom", "shard"), None), P(), P()),
        check_vma=False,
    )
```

profile of v0, /device:TPU:8, one launch (start us, length us, event | category | flops | bytes accessed | tf_op | source)
XLA Modules:
  0.0 480.2 jit_solution(18046370803552838058)
XLA Ops:
  8.2 1.9 gather_fusion.1
  11.0 11.3 %all-to-all-start = ((bf16[32,4,512]{2,1,0:T(4,128)(2,1)}), bf16[32,4,512]{2,1,0:T(4,128)(2,1)S(1)}, u32[]{:S(2)}, u32[]{:S(2)}) async-start(bf16[32,4,512]{2,1,0:T(4,128)(2,1)} %broadcast_select_fusion), calls=%async_computation | async-start | bytes 262144 | tf_op jit(solution)/shard_map/all_to_all | solution.py:32
  23.2 69.5 %all-gather = bf16[256,1,512]{2,1,0:T(2,128)(2,1)S(1)} all-gather(bf16[1,1,512]{2,1,0:T(2,128)(2,1)S(1)} %dynamic-slice_bitcast_fusion.1), channel_id=1, replica_groups=mesh['dom'=8,'shard'=32] {'dom','shard'}, dimensions={0}, use_global_device_ids=true | all-gather | bytes 263168 | tf_op jit(solution)/shard_map/all_gather | solution.py:30
  93.4 42.3 %while.22 = (s32[]{:T(128)}, f32[2,128,512]{2,1,0:T(8,128)S(1)}, s32[2,128,32]{2,1,0:T(8,128)S(1)}, bf16[641,512]{1,0:T(8,128)(2,1)S(1)}, s32[]{:T(128)}) while((s32[]{:T(128)}, f32[2,128,512]{2,1,0:T(8,128)S(1)}, s32[2,128,32]{2,1,0:T(8,128)S(1)}, bf16[641,512]{1,0:T(8,128)(2,1)S(1)}, s32[]{:T(128)}) %tuple.59), condition=%wide.region_2.3_spmd, body=%wide.region_0.0_spmd.sunk | while | flops 4145154 | bytes 13484109 | solution.py:41
  93.5 17.3 %gather_fusion = bf16[4096,512]{1,0:T(8,128)(2,1)} fusion(bf16[641,512]{1,0:T(8,128)(2,1)S(1)} %get-tuple-element.173, s32[4096]{0:T(1024)S(1)} %broadcast_clamp_fusion.2), kind=kCustom, calls=%fused_computation.clone.1 | custom fusion | bytes 8404992 | tf_op jit(solution)/shard_map/while/body/eval_jaxpr/gather | solution.py:41
  110.8 3.7 convert_reduce_fusion.3
  114.6 17.3 %gather_fusion = bf16[4096,512]{1,0:T(8,128)(2,1)} fusion(bf16[641,512]{1,0:T(8,128)(2,1)S(1)} %get-tuple-element.173, s32[4096]{0:T(1024)S(1)} %broadcast_clamp_fusion.2), kind=kCustom, calls=%fused_computation.clone.1 | custom fusion | bytes 8404992 | tf_op jit(solution)/shard_map/while/body/eval_jaxpr/gather | solution.py:41
  132.0 3.7 convert_reduce_fusion.3
  135.8 1.2 multiply_convert_fusion
  137.4 1.3 convolution_bitcast_fusion
  138.7 1.3 fusion.3
  140.1 61.5 %while.23 = (s32[]{:T(128)}, f32[641,512]{1,0:T(8,128)S(1)}, s32[2,128,32]{2,1,0:T(8,128)S(1)}, f32[2,128,512]{2,1,0:T(8,128)S(1)}, s32[]{:T(128)}) while((s32[]{:T(128)}, f32[641,512]{1,0:T(8,128)S(1)}, s32[2,128,32]{2,1,0:T(8,128)S(1)}, f32[2,128,512]{2,1,0:T(8,128)S(1)}, s32[]{:T(128)}) %tuple.61), condition=%wide.region_6.7_spmd, body=%wide.region_4.6_spmd.sunk | while | flops 2109442 | bytes 34455628 | solution.py:63
  140.3 4.3 broadcast_in_dim.68
  144.6 26.2 %scatter_fusion = f32[641,512]{1,0:T(8,128)S(1)} fusion(f32[641,512]{1,0:T(8,128)S(1)} %get-tuple-element.181, s32[4096]{0:T(1024)S(1)} %bitcast.62, f32[4096,512]{1,0:T(8,128)} %bitcast.59), kind=kCustom, calls=%fused_computation.2.clone.1 | custom fusion | flops 2097152 | bytes 25182208 | tf_op jit(solution)/shard_map/while/body/eval_jaxpr/scatter-add | solution.py:60
  171.0 4.3 broadcast_in_dim.68
  175.3 26.3 %scatter_fusion = f32[641,512]{1,0:T(8,128)S(1)} fusion(f32[641,512]{1,0:T(8,128)S(1)} %get-tuple-element.181, s32[4096]{0:T(1024)S(1)} %bitcast.62, f32[4096,512]{1,0:T(8,128)} %bitcast.59), kind=kCustom, calls=%fused_computation.2.clone.1 | custom fusion | flops 2097152 | bytes 25182208 | tf_op jit(solution)/shard_map/while/body/eval_jaxpr/scatter-add | solution.py:60
  201.6 0.8 slice.25
  204.8 7.0 %all-to-all-start.1 = ((bf16[32,4,512]{2,1,0:T(4,128)(2,1)}), bf16[32,4,512]{2,1,0:T(4,128)(2,1)S(1)}, u32[]{:S(2)}, u32[]{:S(2)}) async-start(bf16[32,4,512]{2,1,0:T(4,128)(2,1)} %convert_element_type.38), calls=%async_computation.1 | async-start | bytes 262144 | tf_op jit(solution)/shard_map/all_to_all | solution.py:67
  212.2 10.3 %all-to-all-done.1 = bf16[32,4,512]{2,1,0:T(4,128)(2,1)S(1)} async-done(((bf16[32,4,512]{2,1,0:T(4,128)(2,1)}), bf16[32,4,512]{2,1,0:T(4,128)(2,1)S(1)}, u32[]{:S(2)}, u32[]{:S(2)}) %all-to-all-start.1) | async-done | bytes 131104 | tf_op jit(solution)/shard_map/all_to_all | solution.py:67
  222.7 244.0 %all-reduce.4.cloned.1.call-done = (f32[256,512]{1,0:T(8,128)}, f32[512,512]{0,1:T(8,128)}, f32[512,512]{1,0:T(8,128)}) async-done(((f32[256,512]{1,0:T(8,128)}, f32[512,512]{0,1:T(8,128)}, f32[512,512]{1,0:T(8,128)}), (f32[256,512]{1,0:T(8,128)}, f32[512,512]{0,1:T(8,128)}, f32[512,512]{1,0:T(8,128)})) %all-reduce.4.cloned.1.call-update) | async-done | bytes 2621456
  466.7 1.3 broadcast_select_fusion.1
  468.1 2.5 copy.27
  470.7 1.5 scatter_fusion.1
  472.2 1.0 copy.51
  (79 shorter events, 6.8 us)
Async XLA Ops:
  7.2 128.6 %copy-start = (bf16[512,512]{1,0:T(8,128)(2,1)S(1)}, bf16[512,512]{1,0:T(8,128)(2,1)}, u32[]{:S(2)}) copy-start(bf16[512,512]{1,0:T(8,128)(2,1)} %param.16) | copy-start | bytes 1572868
  7.2 16.0 %copy-start.2 = (bf16[256,512]{1,0:T(8,128)(2,1)S(1)}, bf16[256,512]{1,0:T(8,128)(2,1)}, u32[]{:S(2)}) copy-start(bf16[256,512]{1,0:T(8,128)(2,1)} %param.14) | copy-start | bytes 786436
  7.2 2.9 copy-start.12
  7.2 15.2 %copy-start.8 = (s32[256,32]{0,1:T(8,128)S(1)}, s32[256,32]{0,1:T(8,128)}, u32[]{:S(2)}) copy-start(s32[256,32]{0,1:T(8,128)} %param.18) | copy-start | bytes 98308
  10.0 82.7 %copy-start.5 = (bf16[512,512]{1,0:T(8,128)(2,1)S(1)}, bf16[512,512]{1,0:T(8,128)(2,1)}, u32[]{:S(2)}) copy-start(bf16[512,512]{1,0:T(8,128)(2,1)} %param.15) | copy-start | bytes 1572868
  10.2 0.8 copy-start.9
  11.0 82.1 %all-to-all-start = ((bf16[32,4,512]{2,1,0:T(4,128)(2,1)}), bf16[32,4,512]{2,1,0:T(4,128)(2,1)S(1)}, u32[]{:S(2)}, u32[]{:S(2)}) async-start(bf16[32,4,512]{2,1,0:T(4,128)(2,1)} %broadcast_select_fusion), calls=%async_computation | async-start | bytes 262144 | tf_op jit(solution)/shard_map/all_to_all | solution.py:32
  22.3 444.4 %all-reduce.4.cloned.1.call-start = ((), (), s32[]{:S(2)}) async-start(), calls=%async_computation.2 | async-start | bytes 5242880
  93.3 42.5 %copy-start.14 = (bf16[256,512]{1,0:T(8,128)(2,1)S(1)}, bf16[256,512]{1,0:T(8,128)(2,1)}, u32[]{:S(2)}) copy-start(bf16[256,512]{1,0:T(8,128)(2,1)} %param.17) | copy-start | bytes 786436
  137.0 1.6 copy-start.3
  202.5 0.7 copy-start.11
  202.5 0.9 copy-start.13
  202.5 9.4 %copy-start.4 = (bf16[256,512]{1,0:T(8,128)(2,1)S(1)}, bf16[256,512]{1,0:T(8,128)(2,1)}, u32[]{:S(2)}) copy-start(bf16[256,512]{1,0:T(8,128)(2,1)} %copy-done.3) | copy-start | bytes 786436
  202.5 9.4 %copy-start.6 = (bf16[512,512]{1,0:T(8,128)(2,1)S(1)}, bf16[512,512]{1,0:T(8,128)(2,1)}, u32[]{:S(2)}) copy-start(bf16[512,512]{1,0:T(8,128)(2,1)} %param.15) | copy-start | bytes 1572868
  203.2 19.3 %copy-start.10 = (pred[32,4]{1,0:T(8,128)(4,1)S(1)}, pred[32,4]{1,0:T(8,128)(4,1)}, u32[]{:S(2)}) copy-start(pred[32,4]{1,0:T(8,128)(4,1)} %copy-done.9) | copy-start | bytes 388
  204.8 17.6 %all-to-all-start.1 = ((bf16[32,4,512]{2,1,0:T(4,128)(2,1)}), bf16[32,4,512]{2,1,0:T(4,128)(2,1)S(1)}, u32[]{:S(2)}, u32[]{:S(2)}) async-start(bf16[32,4,512]{2,1,0:T(4,128)(2,1)} %convert_element_type.38), calls=%async_computation.1 | async-start | bytes 262144 | tf_op jit(solution)/shard_map/all_to_all | solution.py:67
  470.7 1.6 copy-start.7
  472.2 1.1 copy-start.1
Sparse Core Ops, SparseCore 0:
  202.6 264.0 all-reduce.3
where the time goes:
time: 481 us; the launch traced here: 480 us
  waiting for transfers between devices  254 us (53%)
  blocking collectives  69.5 us (14%)
  other arithmetic  65.7 us (14%)
  local copies, waits for them, and re-layouts  52.4 us (11%)
  starting transfers between devices  18.3 us (4%)
  between operations  15 us (3%)
    unnamed x2, waiting for transfers between devices  244 us
    all_gather x1, blocking collectives, body(): hubs = lax.all_gather(hub_local, ('dom', 'shard'), axis=0, tiled=True)  69.5 us
    scatter-add x2, other arithmetic, add_block(): return (acc.at[blk.reshape(-1)].add(spread), None)  52.5 us
    gather x2, local copies, waits for them, and re-layouts, body(): table[blk]  34.6 us
    all_to_all x1, starting transfers between devices, body(): lax.all_to_all(outgoing, 'shard', split_axis=0, concat_axis=0, tiled=True)  11.3 us
    all_to_all x1, waiting for transfers between devices, body(): lax.all_to_all(recv_part.astype(jnp.bfloat16), 'shard', split_axis=0, con...  10.3 us
  transfers between devices with their start and end apart: 3, of which 2 were waited for; matrix products, arithmetic and copies ran while one was open for 1% of the time, Pallas kernels for 0%

commit v1 on v0

--- a/solution.py
+++ b/solution.py
@@ -27,7 +27,12 @@
     cap = routes.shape[1]
     live = jnp.arange(cap)[None, :] < counts[:, None]
     hub_local = features[hub_slots]
-    hubs = lax.all_gather(hub_local, ("dom", "shard"), axis=0, tiled=True)
+    hubs = jnp.concatenate(
+        lax.all_to_all(
+            jnp.stack([hub_local] * lax.axis_size(("dom", "shard"))), ("dom", "shard"), 0, 0
+        ),
+        axis=0,
+    )
     outgoing = jnp.where(live[:, :, None], features[routes], jnp.zeros((), jnp.bfloat16))
     incoming = lax.all_to_all(outgoing, "shard", split_axis=0, concat_axis=0, tiled=True)
     hub_count = hubs.shape[0]

time: 481 us -> 437 us (0.909)
  blocking collectives: 69.5 us -> 0 us
  waiting for transfers between devices: 254 us -> 272 us
    all_gather x1 -> x0, blocking collectives: 69.5 us -> none  [body(): hubs = lax.all_gather(hub_local, ('dom', 'shard'), axis=0, tiled=True)]
    all_to_all x0 -> x1, waiting for transfers between devices: none -> 14.2 us  [body(): lax.all_to_all(jnp.stack([hub_local] * lax.axis_size(('dom', 'shard'))),...]
    all_to_all x0 -> x1, starting transfers between devices: none -> 7.4 us  [body(): lax.all_to_all(jnp.stack([hub_local] * lax.axis_size(('dom', 'shard'))),...]
    all_to_all x1, waiting for transfers between devices: 0.01 us -> 5.68 us  [body(): lax.all_to_all(outgoing, 'shard', split_axis=0, concat_axis=0, tiled=True)]
  transfers between devices with their start and end apart: 3 -> 4, of which waited for: 2 -> 4; matrix products, arithmetic and copies ran while one was open for 1% -> 1% of each run, Pallas kernels for 0% -> 0%
where the time goes in v1:
time: 437 us
  waiting for transfers between devices  272 us (62%)
  other arithmetic  67.8 us (16%)
  local copies, waits for them, and re-layouts  54.1 us (12%)
  starting transfers between devices  22.7 us (5%)
  between operations  15.1 us (3%)
  matrix products  4.76 us (1%)
    unnamed x2, waiting for transfers between devices  242 us
    scatter-add x2, other arithmetic, add_block(): return (acc.at[blk.reshape(-1)].add(spread), None)  52.5 us
    gather x2, local copies, waits for them, and re-layouts, body(): table[blk]  34.5 us
    all_to_all x1, waiting for transfers between devices, body(): lax.all_to_all(jnp.stack([hub_local] * lax.axis_size(('dom', 'shard'))),...  14.2 us
    all_to_all x1, starting transfers between devices, body(): lax.all_to_all(outgoing, 'shard', split_axis=0, concat_axis=0, tiled=True)  11.4 us
    all_to_all x1, waiting for transfers between devices, body(): lax.all_to_all(recv_part.astype(jnp.bfloat16), 'shard', split_axis=0, con...  10.5 us
  transfers between devices with their start and end apart: 4, of which 4 were waited for; matrix products, arithmetic and copies ran while one was open for 1% of the time, Pallas kernels for 0%

profile of v1, /device:TPU:8, one launch (start us, length us, event | category | flops | bytes accessed | tf_op | source)
XLA Modules:
  0.0 436.9 jit_solution(1074457856630310040)
XLA Ops:
  8.2 1.9 gather_fusion.1
  11.0 11.4 %all-to-all-start.1 = ((bf16[32,4,512]{2,1,0:T(4,128)(2,1)}), bf16[32,4,512]{2,1,0:T(4,128)(2,1)S(1)}, u32[]{:S(2)}, u32[]{:S(2)}) async-start(bf16[32,4,512]{2,1,0:T(4,128)(2,1)} %broadcast_select_fusion), calls=%async_computation.1 | async-start | bytes 262144 | tf_op jit(solution)/shard_map/all_to_all | solution.py:37
  24.0 2.3 reduce.10
  27.0 5.7 %all-to-all-done.1 = bf16[32,4,512]{2,1,0:T(4,128)(2,1)S(1)} async-done(((bf16[32,4,512]{2,1,0:T(4,128)(2,1)}), bf16[32,4,512]{2,1,0:T(4,128)(2,1)S(1)}, u32[]{:S(2)}, u32[]{:S(2)}) %all-to-all-start.1) | async-done | bytes 131104 | tf_op jit(solution)/shard_map/all_to_all | solution.py:37
  32.7 7.4 %all-to-all-start = ((bf16[256,2,256]{2,1,0:T(2,128)(2,1)}), bf16[256,2,256]{2,1,0:T(2,128)(2,1)S(1)}, u32[]{:S(2)}, u32[]{:S(2)}) async-start(bf16[256,2,256]{2,1,0:T(2,128)(2,1)} %reshape.270), calls=%async_computation | async-start | bytes 524288 | tf_op jit(solution)/shard_map/all_to_all | solution.py:31
  40.7 14.2 %all-to-all-done = bf16[256,2,256]{2,1,0:T(2,128)(2,1)S(1)} async-done(((bf16[256,2,256]{2,1,0:T(2,128)(2,1)}), bf16[256,2,256]{2,1,0:T(2,128)(2,1)S(1)}, u32[]{:S(2)}, u32[]{:S(2)}) %all-to-all-start) | async-done | bytes 262176 | tf_op jit(solution)/shard_map/all_to_all | solution.py:31
  55.3 42.2 %while.22 = (s32[]{:T(128)}, f32[2,128,512]{2,1,0:T(8,128)S(1)}, s32[2,128,32]{2,1,0:T(8,128)S(1)}, bf16[641,512]{1,0:T(8,128)(2,1)S(1)}, s32[]{:T(128)}) while((s32[]{:T(128)}, f32[2,128,512]{2,1,0:T(8,128)S(1)}, s32[2,128,32]{2,1,0:T(8,128)S(1)}, bf16[641,512]{1,0:T(8,128)(2,1)S(1)}, s32[]{:T(128)}) %tuple.59), condition=%wide.region_2.3_spmd, body=%wide.region_0.0_spmd.sunk | while | flops 4145154 | bytes 13484109 | solution.py:46
  55.5 17.3 %gather_fusion = bf16[4096,512]{1,0:T(8,128)(2,1)} fusion(bf16[641,512]{1,0:T(8,128)(2,1)S(1)} %get-tuple-element.173, s32[4096]{0:T(1024)S(1)} %broadcast_clamp_fusion.2), kind=kCustom, calls=%fused_computation.clone.1 | custom fusion | bytes 8404992 | tf_op jit(solution)/shard_map/while/body/eval_jaxpr/gather | solution.py:46
  72.7 3.7 convert_reduce_fusion.3
  76.6 17.3 %gather_fusion = bf16[4096,512]{1,0:T(8,128)(2,1)} fusion(bf16[641,512]{1,0:T(8,128)(2,1)S(1)} %get-tuple-element.173, s32[4096]{0:T(1024)S(1)} %broadcast_clamp_fusion.2), kind=kCustom, calls=%fused_computation.clone.1 | custom fusion | bytes 8404992 | tf_op jit(solution)/shard_map/while/body/eval_jaxpr/gather | solution.py:46
  93.9 3.7 convert_reduce_fusion.3
  99.3 1.3 convolution_bitcast_fusion
  100.6 1.3 fusion.3
  102.0 61.5 %while.23 = (s32[]{:T(128)}, f32[641,512]{1,0:T(8,128)S(1)}, s32[2,128,32]{2,1,0:T(8,128)S(1)}, f32[2,128,512]{2,1,0:T(8,128)S(1)}, s32[]{:T(128)}) while((s32[]{:T(128)}, f32[641,512]{1,0:T(8,128)S(1)}, s32[2,128,32]{2,1,0:T(8,128)S(1)}, f32[2,128,512]{2,1,0:T(8,128)S(1)}, s32[]{:T(128)}) %tuple.61), condition=%wide.region_6.7_spmd, body=%wide.region_4.6_spmd.sunk | while | flops 2109442 | bytes 34455628 | solution.py:68
  102.2 4.3 broadcast_in_dim.68
  106.5 26.2 %scatter_fusion = f32[641,512]{1,0:T(8,128)S(1)} fusion(f32[641,512]{1,0:T(8,128)S(1)} %get-tuple-element.181, s32[4096]{0:T(1024)S(1)} %bitcast.60, f32[4096,512]{1,0:T(8,128)} %bitcast.57), kind=kCustom, calls=%fused_computation.2.clone.1 | custom fusion | flops 2097152 | bytes 25182208 | tf_op jit(solution)/shard_map/while/body/eval_jaxpr/scatter-add | solution.py:65
  132.9 4.3 broadcast_in_dim.68
  137.2 26.3 %scatter_fusion = f32[641,512]{1,0:T(8,128)S(1)} fusion(f32[641,512]{1,0:T(8,128)S(1)} %get-tuple-element.181, s32[4096]{0:T(1024)S(1)} %bitcast.60, f32[4096,512]{1,0:T(8,128)} %bitcast.57), kind=kCustom, calls=%fused_computation.2.clone.1 | custom fusion | flops 2097152 | bytes 25182208 | tf_op jit(solution)/shard_map/while/body/eval_jaxpr/scatter-add | solution.py:65
  166.6 3.9 all-to-all-start.2
  170.9 10.5 %all-to-all-done.2 = bf16[32,4,512]{2,1,0:T(4,128)(2,1)S(1)} async-done(((bf16[32,4,512]{2,1,0:T(4,128)(2,1)}), bf16[32,4,512]{2,1,0:T(4,128)(2,1)S(1)}, u32[]{:S(2)}, u32[]{:S(2)}) %all-to-all-start.2) | async-done | bytes 131104 | tf_op jit(solution)/shard_map/all_to_all | solution.py:72
  181.6 241.9 %all-reduce.4.cloned.1.call-done = (f32[256,512]{1,0:T(8,128)}, f32[512,512]{0,1:T(8,128)}, f32[512,512]{1,0:T(8,128)}) async-done(((f32[256,512]{1,0:T(8,128)}, f32[512,512]{0,1:T(8,128)}, f32[512,512]{1,0:T(8,128)}), (f32[256,512]{1,0:T(8,128)}, f32[512,512]{0,1:T(8,128)}, f32[512,512]{1,0:T(8,128)})) %all-reduce.4.cloned.1.call-update) | async-done | bytes 2621456
  423.5 1.3 broadcast_select_fusion.1
  424.8 2.5 copy.27
  427.3 1.5 scatter_fusion.1
  (85 shorter events, 11.6 us)
Async XLA Ops:
  7.2 90.5 %copy-start = (bf16[512,512]{1,0:T(8,128)(2,1)S(1)}, bf16[512,512]{1,0:T(8,128)(2,1)}, u32[]{:S(2)}) copy-start(bf16[512,512]{1,0:T(8,128)(2,1)} %param.16) | copy-start | bytes 1572868
  7.2 16.0 %copy-start.2 = (bf16[256,512]{1,0:T(8,128)(2,1)S(1)}, bf16[256,512]{1,0:T(8,128)(2,1)}, u32[]{:S(2)}) copy-start(bf16[256,512]{1,0:T(8,128)(2,1)} %param.14) | copy-start | bytes 786436
  7.2 2.9 copy-start.12
  10.2 0.8 copy-start.9
  11.0 29.2 %copy-start.8 = (s32[256,32]{0,1:T(8,128)S(1)}, s32[256,32]{0,1:T(8,128)}, u32[]{:S(2)}) copy-start(s32[256,32]{0,1:T(8,128)} %param.18) | copy-start | bytes 98308
  11.0 21.7 %all-to-all-start.1 = ((bf16[32,4,512]{2,1,0:T(4,128)(2,1)}), bf16[32,4,512]{2,1,0:T(4,128)(2,1)S(1)}, u32[]{:S(2)}, u32[]{:S(2)}) async-start(bf16[32,4,512]{2,1,0:T(4,128)(2,1)} %broadcast_select_fusion), calls=%async_computation.1 | async-start | bytes 262144 | tf_op jit(solution)/shard_map/all_to_all | solution.py:37
  22.4 17.9 %copy-start.5 = (bf16[512,512]{1,0:T(8,128)(2,1)S(1)}, bf16[512,512]{1,0:T(8,128)(2,1)}, u32[]{:S(2)}) copy-start(bf16[512,512]{1,0:T(8,128)(2,1)} %param.15) | copy-start | bytes 1572868
  32.7 22.2 %all-to-all-start = ((bf16[256,2,256]{2,1,0:T(2,128)(2,1)}), bf16[256,2,256]{2,1,0:T(2,128)(2,1)S(1)}, u32[]{:S(2)}, u32[]{:S(2)}) async-start(bf16[256,2,256]{2,1,0:T(2,128)(2,1)} %reshape.270), calls=%async_computation | async-start | bytes 524288 | tf_op jit(solution)/shard_map/all_to_all | solution.py:31
  40.1 383.4 %all-reduce.4.cloned.1.call-start = ((), (), s32[]{:S(2)}) async-start(), calls=%async_computation.3 | async-start | bytes 5242880
  55.3 42.4 %copy-start.14 = (bf16[256,512]{1,0:T(8,128)(2,1)S(1)}, bf16[256,512]{1,0:T(8,128)(2,1)}, u32[]{:S(2)}) copy-start(bf16[256,512]{1,0:T(8,128)(2,1)} %param.17) | copy-start | bytes 786436
  98.9 1.6 copy-start.3
  164.4 0.7 copy-start.11
  164.4 0.9 copy-start.13
  164.4 6.1 %copy-start.4 = (bf16[256,512]{1,0:T(8,128)(2,1)S(1)}, bf16[256,512]{1,0:T(8,128)(2,1)}, u32[]{:S(2)}) copy-start(bf16[256,512]{1,0:T(8,128)(2,1)} %copy-done.3) | copy-start | bytes 786436
  164.4 6.2 %copy-start.6 = (bf16[512,512]{1,0:T(8,128)(2,1)S(1)}, bf16[512,512]{1,0:T(8,128)(2,1)}, u32[]{:S(2)}) copy-start(bf16[512,512]{1,0:T(8,128)(2,1)} %param.15) | copy-start | bytes 1572868
  165.1 16.2 %copy-start.10 = (pred[32,4]{1,0:T(8,128)(4,1)S(1)}, pred[32,4]{1,0:T(8,128)(4,1)}, u32[]{:S(2)}) copy-start(pred[32,4]{1,0:T(8,128)(4,1)} %copy-done.9) | copy-start | bytes 388
  166.6 14.7 %all-to-all-start.2 = ((bf16[32,4,512]{2,1,0:T(4,128)(2,1)}), bf16[32,4,512]{2,1,0:T(4,128)(2,1)S(1)}, u32[]{:S(2)}, u32[]{:S(2)}) async-start(bf16[32,4,512]{2,1,0:T(4,128)(2,1)} %convert_element_type.38), calls=%async_computation.2 | async-start | bytes 262144 | tf_op jit(solution)/shard_map/all_to_all | solution.py:72
  427.3 1.6 copy-start.7
  428.9 1.1 copy-start.1
Sparse Core Ops, SparseCore 0:
  164.5 258.9 all-reduce.3
